TPU v7x, 32 devices: a whole 2x2x4 slice. The times are simulated.
32 devices in a mesh: row: 16 (over z, x, core), col: 2 (over y).
Axes of the slice: x: 2, y: 2, z: 4, core: 2. Of those that a mesh axis runs over, the one named last changes fastest.
Arguments:
- row_features: bfloat16 [256, 256], P(('row', 'col')), may hold values from -6 to 6
- col_features: bfloat16 [512, 256], P(('col', 'row')), may hold values from -6 to 6
- row_proj: bfloat16 [256, 64], replicated, may hold values from -0.375 to 0.375
- col_proj: bfloat16 [256, 64], replicated, may hold values from -0.375 to 0.375
- pair_weight: bfloat16 [2, 3, 3, 64, 64], replicated, may hold values from -0.1875 to 0.1875
- pair_bias: float32 [64], replicated, may hold values from -4 to 4
- conv_weight: bfloat16 [3, 3, 64, 64], replicated, may hold values from -0.25 to 0.25
- dilations: int32 [2], replicated, may hold values from 1 to 8, as said below
- cotangent: bfloat16 [64, 256, 512], P(None, 'row', 'col'), may hold values from -6 to 6
Outputs:
- pair_out: bfloat16 [64, 256, 512], P(None, 'row', 'col')
- grad_row_features: float32 [256, 256], P(('row', 'col'))
- grad_col_features: float32 [512, 256], P(('col', 'row'))
- grad_row_proj: float32 [256, 64], replicated
- grad_col_proj: float32 [256, 64], replicated
- grad_pair_weight: float32 [2, 3, 3, 64, 64], replicated
- grad_pair_bias: float32 [64], replicated
- grad_conv_weight: float32 [3, 3, 64, 64], replicated
Inputs may be any that keep to these rules, and one draw needn't show every extreme that they name: One of the two dilations equals 8.
All inputs are finite; a program needn't handle non-finite values.
Results may differ from a plain program's by a relative error of at most 0.0054.
Values may be sent and summed in bfloat16 or wider, within the bound.
No kernel may reach another device: no remote copies, remote signals or barrier semaphores. Data moves between devices by JAX's collectives and lax.ppermute only.
A program may use at most 64 MiB of HBM per device.

v0:
```python
import jax
import jax.numpy as jnp
from jax import lax
from jax.sharding import PartitionSpec as P

MAX_DILATION = 8


def padded_2(value, sides, width):
    for axis, dim in sides:
        devices, length = (lax.axis_size(axis), value.shape[dim])
        up = [(i, (i + 1) % devices) for i in range(devices - 1)]
        down = [(j, i) for i, j in up]
        last = lax.slice_in_dim(value, length - width, length, axis=dim)
        leading = lax.slice_in_dim(value, 0, width, axis=dim)
        before = lax.ppermute(last, axis, up)
        after = lax.ppermute(leading, axis, down)
        value = jnp.concatenate([before, value, after], axis=dim)
    return value


def project(features, weight):
    return jnp.dot(features, weight, preferred_element_type=jnp.float32).astype(jnp.bfloat16)


def line_terms(padded, weights, dilation, count, offset):
    shifted = jnp.stack(
        [
            lax.dynamic_slice_in_dim(padded, offset + (tap_idx - 1) * dilation, count, 0)
            for tap_idx in range(3)
        ]
    )
    return jnp.einsum("kip,kqpo->qio", shifted, weights, preferred_element_type=jnp.float32)


def line_valid(first_cell, count, cell_limit, dilation):
    cells = first_cell + jnp.arange(count, dtype=jnp.int32)
    columns = [
        (cells + (tap_idx - 1) * dilation >= 0) & (cells + (tap_idx - 1) * dilation < cell_limit)
        for tap_idx in range(3)
    ]
    return jnp.stack(columns, axis=1).astype(jnp.float32)


def pair_field(row_terms, col_terms, row_valid, col_valid, bias):
    from_rows = jnp.einsum("jq,qic->cij", col_valid, row_terms, precision=lax.Precision.HIGHEST)
    from_cols = jnp.einsum("ik,kjc->cij", row_valid, col_terms, precision=lax.Precision.HIGHEST)
    return from_rows + from_cols + bias[:, None, None]


def window_at(padded, row_index, col_index, rows, cols):
    anchor = jnp.zeros((), jnp.int32)
    return lax.dynamic_slice(padded, (anchor, row_index, col_index), (padded.shape[0], rows, cols))


def conv_taps(padded, weight, dilation, rows, cols, margin):
    result = jnp.zeros((weight.shape[3], rows, cols), jnp.float32)
    for tap_row in range(3):
        for tap_col in range(3):
            window = window_at(
                padded,
                margin + (tap_row - 1) * dilation,
                margin + (tap_col - 1) * dilation,
                rows,
                cols,
            )
            result = result + jnp.einsum(
                "co,cij->oij", weight[tap_row, tap_col], window, preferred_element_type=jnp.float32
            )
    return result


def back_taps(padded, weight, dilation, rows, cols, margin):
    result = jnp.zeros((weight.shape[2], rows, cols), jnp.float32)
    for tap_row in range(3):
        for tap_col in range(3):
            window = window_at(
                padded,
                margin - (tap_row - 1) * dilation,
                margin - (tap_col - 1) * dilation,
                rows,
                cols,
            )
            result = result + jnp.einsum(
                "co,oij->cij", weight[tap_row, tap_col], window, preferred_element_type=jnp.float32
            )
    return result


def tap_grads(hidden_pad, grads, dilation, rows, cols, margin):
    stacked = []
    for tap_row in range(3):
        line_list = []
        for tap_col in range(3):
            window = window_at(
                hidden_pad,
                margin + (tap_row - 1) * dilation,
                margin + (tap_col - 1) * dilation,
                rows,
                cols,
            )
            line_list.append(
                jnp.einsum("cij,oij->co", window, grads, preferred_element_type=jnp.float32)
            )
        stacked.append(jnp.stack(line_list))
    return jnp.stack(stacked)


def shards(
    row_features,
    col_features,
    row_proj,
    col_proj,
    pair_weight,
    pair_bias,
    conv_weight,
    dilations,
    cotangent,
):
    first_rate = dilations[0]
    second_rate = dilations[1]
    margin = MAX_DILATION
    row_count = lax.axis_size("row")
    col_count = lax.axis_size("col")
    row_place = lax.axis_index("row")
    col_place = lax.axis_index("col")
    rows_here = cotangent.shape[1]
    cols_here = cotangent.shape[2]
    row_start = row_place * rows_here
    col_start = col_place * cols_here
    row_limit = rows_here * row_count
    col_limit = cols_here * col_count
    row_piece = row_features.shape[0]
    col_piece = col_features.shape[0]
    rows_a = lax.all_gather(project(row_features, row_proj), "col", axis=0, tiled=True)
    cols_b = lax.all_gather(project(col_features, col_proj), "row", axis=0, tiled=True)
    pad_extra = 0
    a_pad = padded_2(rows_a, (("row", 0),), MAX_DILATION)
    b_pad = padded_2(cols_b, (("col", 0),), MAX_DILATION)
    row_terms = line_terms(
        a_pad, pair_weight[0], first_rate, rows_here + 2 * pad_extra, margin - pad_extra
    )
    col_terms = line_terms(
        b_pad,
        jnp.swapaxes(pair_weight[1], 0, 1),
        first_rate,
        cols_here + 2 * pad_extra,
        margin - pad_extra,
    )
    row_valid = line_valid(row_start - pad_extra, rows_here + 2 * pad_extra, row_limit, first_rate)
    col_valid = line_valid(col_start - pad_extra, cols_here + 2 * pad_extra, col_limit, first_rate)
    pre_act = pair_field(row_terms, col_terms, row_valid, col_valid, pair_bias)
    hidden_own = jax.nn.silu(pre_act).astype(jnp.bfloat16)
    hidden = padded_2(hidden_own, (("row", 1), ("col", 2)), MAX_DILATION)
    conv_mixed = conv_taps(hidden, conv_weight, second_rate, rows_here, cols_here, margin)
    pair_out = (hidden_own.astype(jnp.float32) + conv_mixed).astype(jnp.bfloat16)
    grad_pad = padded_2(cotangent, (("row", 1), ("col", 2)), MAX_DILATION)
    d_hidden = cotangent.astype(jnp.float32) + back_taps(
        grad_pad, conv_weight, second_rate, rows_here, cols_here, margin
    )
    conv_grad = tap_grads(hidden, cotangent, second_rate, rows_here, cols_here, margin)
    sigmoid_own = jax.nn.sigmoid(pre_act)
    d_pre = d_hidden * sigmoid_own * (1.0 + pre_act * (1.0 - sigmoid_own))
    bias_grad = jnp.sum(d_pre, axis=(1, 2))
    row_valid_own = line_valid(row_start, rows_here, row_limit, first_rate)
    col_valid_own = line_valid(col_start, cols_here, col_limit, first_rate)
    row_part = jnp.einsum("jq,cij->qic", col_valid_own, d_pre, precision=lax.Precision.HIGHEST)
    col_part = jnp.einsum("ik,cij->kjc", row_valid_own, d_pre, precision=lax.Precision.HIGHEST)
    row_sums = lax.psum(row_part, "col")
    col_sums = lax.psum(col_part, "row")
    back_rows = jnp.einsum(
        "qio,kqpo->kip",
        row_sums,
        pair_weight[0].astype(jnp.float32),
        precision=lax.Precision.HIGHEST,
    )
    back_cols = jnp.einsum(
        "kjo,kqpo->qjp",
        col_sums,
        pair_weight[1].astype(jnp.float32),
        precision=lax.Precision.HIGHEST,
    )
    rows_back_pad = padded_2(back_rows, (("row", 1),), MAX_DILATION)
    cols_back_pad = padded_2(back_cols, (("col", 1),), MAX_DILATION)
    row_own = col_place * row_piece
    col_own = row_place * col_piece
    d_rows = sum(
        (
            lax.dynamic_slice_in_dim(
                rows_back_pad[tap_idx], margin + row_own - (tap_idx - 1) * first_rate, row_piece, 0
            )
            for tap_idx in range(3)
        )
    )
    d_cols = sum(
        (
            lax.dynamic_slice_in_dim(
                cols_back_pad[tap_idx], margin + col_own - (tap_idx - 1) * first_rate, col_piece, 0
            )
            for tap_idx in range(3)
        )
    )
    d_rows = d_rows.astype(jnp.bfloat16)
    d_cols = d_cols.astype(jnp.bfloat16)
    grad_row_features = jnp.dot(d_rows, row_proj.T, preferred_element_type=jnp.float32)
    grad_col_features = jnp.dot(d_cols, col_proj.T, preferred_element_type=jnp.float32)
    grad_row_proj = jnp.dot(row_features.T, d_rows, preferred_element_type=jnp.float32)
    grad_col_proj = jnp.dot(col_features.T, d_cols, preferred_element_type=jnp.float32)
    row_shifted = jnp.stack(
        [
            lax.dynamic_slice_in_dim(
                a_pad, margin + row_own + (tap_idx - 1) * first_rate, row_piece, 0
            )
            for tap_idx in range(3)
        ]
    )
    col_shifted = jnp.stack(
        [
            lax.dynamic_slice_in_dim(
                b_pad, margin + col_own + (tap_idx - 1) * first_rate, col_piece, 0
            )
            for tap_idx in range(3)
        ]
    )
    row_sums_own = lax.dynamic_slice_in_dim(row_sums, row_own, row_piece, 1)
    col_sums_own = lax.dynamic_slice_in_dim(col_sums, col_own, col_piece, 1)
    grad_row_pair = jnp.einsum(
        "kip,qio->kqpo",
        row_shifted.astype(jnp.float32),
        row_sums_own,
        precision=lax.Precision.HIGHEST,
    )
    grad_col_pair = jnp.einsum(
        "qjp,kjo->kqpo",
        col_shifted.astype(jnp.float32),
        col_sums_own,
        precision=lax.Precision.HIGHEST,
    )
    summed = lax.psum(
        (
            grad_row_proj,
            grad_col_proj,
            jnp.stack([grad_row_pair, grad_col_pair]),
            bias_grad,
            conv_grad,
        ),
        ("row", "col"),
    )
    return (
        pair_out,
        grad_row_features,
        grad_col_features,
        summed[0],
        summed[1],
        summed[2],
        summed[3],
        summed[4],
    )


def solution(mesh):
    return jax.shard_map(
        shards,
        mesh=mesh,
        in_specs=(
            P(("row", "col"), None),
            P(("col", "row"), None),
            P(),
            P(),
            P(),
            P(),
            P(),
            P(),
            P(None, "row", "col"),
        ),
        out_specs=(
            P(None, "row", "col"),
            P(("row", "col"), None),
            P(("col", "row"), None),
            P(),
            P(),
            P(),
            P(),
            P(),
        ),
        check_vma=False,
    )
```

profile of v0, /device:TPU:0, one launch (start us, length us, event | category | flops | bytes accessed | tf_op | source)
XLA Modules:
  0.0 352.3 jit_solution(3747171923452874970)
XLA Ops:
  7.9 0.8 convolution_convert_fusion
  8.7 23.3 %all_gather.7 = bf16[256,64]{1,0:T(8,128)(2,1)S(1)} all-gather(bf16[16,64]{1,0:T(8,128)(2,1)S(1)} %convolution_convert_fusion), channel_id=1, replica_groups=mesh['row'=16,'col'=2] {'row'}, dimensions={0}, use_global_device_ids=true | all-gather | bytes 34816 | tf_op jit(solution)/shard_map/all_gather | solution.py:136
  32.0 3.4 collective-permute-start.2
  35.4 1.3 collective-permute-start.3
  36.7 0.9 convolution_convert_fusion.1
  37.6 5.0 %all_gather.6 = bf16[16,64]{1,0:T(8,128)(2,1)S(1)} all-gather(bf16[8,64]{1,0:T(8,128)(2,1)S(1)} %convolution_convert_fusion.1), channel_id=1, replica_groups=mesh['row'=16,'col'=2] {'col'}, dimensions={0}, use_global_device_ids=true | all-gather | bytes 3072 | tf_op jit(solution)/shard_map/all_gather | solution.py:135
  42.6 1.3 collective-permute-start
  43.9 1.3 collective-permute-start.1
  45.2 1.1 fusion.195
  46.3 0.8 copy.143
  47.0 3.7 %collective-permute-start.8 = (bf16[64,8,256]{2,0,1:T(8,128)(2,1)}, bf16[64,8,256]{2,0,1:T(8,128)(2,1)}, u32[]{:S(2)}, u32[]{:S(2)}) collective-permute-start(bf16[64,8,256]{2,0,1:T(8,128)(2,1)} %copy.143), channel_id=1, source_target_pairs={{0,2},{2,4},{4,6},{6,8},{8,10},{10,12},{12,14},{14,16},{16,18},{18... | collective-permute-start | bytes 786440 | tf_op jit(solution)/shard_map/ppermute | solution.py:16
  63.2 1.0 fusion.85
  64.3 1.3 collective-permute-start.9
  67.0 1.4 multiply_convert_fusion
  68.8 3.0 collective-permute-start.4
  71.8 1.3 collective-permute-start.5
  73.5 1.0 constant_dynamic-update-slice_fusion.8
  75.0 4.0 %collective-permute-start.10 = (bf16[64,32,8]{2,0,1:T(8,128)(2,1)S(1)}, bf16[64,32,8]{2,0,1:T(8,128)(2,1)S(1)}, u32[]{:S(2)}, u32[]{:S(2)}) collective-permute-start(bf16[64,32,8]{2,0,1:T(8,128)(2,1)S(1)} %get-tuple-element.20), channel_id=1, source_target_pairs={{0,1},{2,3},{4,5},{6,7},{8,9},{10,11},{12,13},{14,15},{16,17},{18,... | collective-permute-start | bytes 98312 | tf_op jit(solution)/shard_map/ppermute | solution.py:16
  79.0 1.3 collective-permute-start.11
  80.4 1.2 fusion.194
  81.7 5.4 %collective-permute-start.6 = (bf16[64,32,8]{2,0,1:T(8,128)(2,1)}, bf16[64,32,8]{2,0,1:T(8,128)(2,1)}, u32[]{:S(2)}, u32[]{:S(2)}) collective-permute-start(bf16[64,32,8]{2,0,1:T(8,128)(2,1)} %get-tuple-element.22), channel_id=1, source_target_pairs={{0,1},{2,3},{4,5},{6,7},{8,9},{10,11},{12,13},{14,15},{16,17},{18,... | collective-permute-start | bytes 98312 | tf_op jit(solution)/shard_map/ppermute | solution.py:16
  87.1 1.5 collective-permute-start.7
  88.6 2.0 collective-permute-done.10
  90.5 4.7 %collective-permute-done.11 = bf16[64,32,8]{2,0,1:T(8,128)(2,1)S(1)} collective-permute-done((bf16[64,32,8]{2,0,1:T(8,128)(2,1)S(1)}, bf16[64,32,8]{2,0,1:T(8,128)(2,1)S(1)}, u32[]{:S(2)}, u32[]{:S(2)}) %collective-permute-start.11) | collective-permute-done | bytes 32800 | tf_op jit(solution)/shard_map/ppermute | solution.py:17
  95.2 1.1 pad_maximum_fusion.1
  99.2 1.0 fusion.204
  100.2 1.8 convolution_bitcast_fusion.7
  103.0 8.6 %psum.49 = f32[3,16,64]{1,0,2:T(4,128)S(1)} all-reduce(f32[3,16,64]{1,0,2:T(4,128)S(1)} %bitcast.308), channel_id=1, replica_groups=mesh['row'=16,'col'=2] {'col'}, use_global_device_ids=true, to_apply=%region_0.1 | all-reduce | flops 3072 | bytes 24576 | tf_op jit(solution)/shard_map/psum | solution.py:169
  111.9 1.2 convolution_bitcast_fusion.21
  113.1 1.5 collective-permute-start.12
  114.6 1.3 collective-permute-start.13
  116.2 47.7 %psum.54 = f32[64]{0:T(128)} all-reduce(f32[64]{0:T(128)S(1)} %get-tuple-element.56), channel_id=1, replica_groups=mesh['row'=16,'col'=2] {'row','col'}, use_global_device_ids=true, to_apply=%region_6.7 | all-reduce | flops 64 | bytes 512 | tf_op jit(solution)/shard_map/psum | solution.py:239
  163.9 2.2 pad_maximum_fusion
  174.3 1.1 copy.58
  175.5 0.8 convolution_bitcast_fusion.10
  176.3 19.0 %all-reduce.4.cloned.1.call-done = f32[3,256,64]{1,0,2:T(4,128)} async-done(((f32[3,256,64]{1,0,2:T(4,128)}), f32[3,256,64]{1,0,2:T(4,128)}) %all-reduce.4.cloned.1.call-update) | async-done | bytes 196624 | tf_op jit(solution)/shard_map/psum | solution.py:170
  195.3 1.0 constant_dynamic-slice_fusion.3
  196.4 1.3 convolution_bitcast_fusion.8
  197.8 3.5 collective-permute-start.14
  201.3 1.3 collective-permute-start.15
  203.0 0.9 pad_maximum_fusion.3
  203.8 4.1 %collective-permute-done.15 = f32[3,8,64]{1,2,0:T(8,128)S(1)} collective-permute-done((f32[3,8,64]{1,2,0:T(8,128)S(1)}, f32[3,8,64]{1,2,0:T(8,128)S(1)}, u32[]{:S(2)}, u32[]{:S(2)}) %collective-permute-start.15) | collective-permute-done | bytes 6176 | tf_op jit(solution)/shard_map/ppermute | solution.py:17
  208.2 0.8 convolution_bitcast_fusion.9
  209.8 0.8 fusion.206
  210.5 129.1 %all-reduce.6.cloned.1.call-done = (f32[256,64]{0,1:T(8,128)}, f32[256,64]{0,1:T(8,128)}, f32[2,3,3,64,64]{3,4,1,2,0:T(8,128)}, f32[3,3,64,64]{3,2,1,0:T(8,128)}) async-done(((f32[256,64]{0,1:T(8,128)}, f32[256,64]{0,1:T(8,128)}, f32[2,3,3,64,64]{3,4,1,2,0:T(8,128)}, f32[3,3,64,64]{3,2,1,0:T(8,128)}), (f32[256,64]{0,1:T(8,128)}, f32[256,64]{0,1:T(8,128)}, f32[2,3,3,64,64]{3,4,1,2,0:T(8,128)}, ...) | async-done | bytes 573456 | tf_op jit(solution)/shard_map/psum | solution.py:239
  339.6 2.1 copy.59
  341.8 1.5 copy.158
  343.2 1.5 copy.159
  (117 shorter events, 20.5 us)
Async XLA Ops:
  7.2 0.8 copy-start
  7.2 56.0 %copy-start.1 = (bf16[64,16,256]{2,1,0:T(8,128)(2,1)S(1)}, bf16[64,16,256]{2,1,0:T(8,128)(2,1)}, u32[]{:S(2)}) copy-start(bf16[64,16,256]{2,1,0:T(8,128)(2,1)} %param.17) | copy-start | bytes 1572868
  7.2 43.5 %copy-start.12 = (s32[2]{0:T(128)S(1)}, s32[2]{0:T(128)}, u32[]{:S(2)}) copy-start(s32[2]{0:T(128)} %param.16) | copy-start | bytes 28
  7.2 188.1 %all-reduce.4.cloned.1.call-start = ((), (), s32[]{:S(2)}) async-start(), calls=%async_computation | async-start | bytes 524288 | tf_op jit(solution)/shard_map/psum | solution.py:170
  32.0 32.3 %collective-permute-start.2 = (bf16[8,64]{1,0:T(8,128)(2,1)S(1)}, bf16[8,64]{1,0:T(8,128)(2,1)S(1)}, u32[]{:S(2)}, u32[]{:S(2)}) collective-permute-start(bf16[8,64]{1,0:T(8,128)(2,1)S(1)} %get-tuple-element.39), channel_id=1, source_target_pairs={{0,1},{2,3},{4,5},{6,7},{8,9},{10,11},{12,13},{14,15},{16,17},{18,... | collective-permute-start | bytes 3080 | tf_op jit(solution)/shard_map/ppermute | solution.py:16
  35.4 30.3 %collective-permute-start.3 = (bf16[8,64]{1,0:T(8,128)(2,1)S(1)}, bf16[8,64]{1,0:T(8,128)(2,1)S(1)}, u32[]{:S(2)}, u32[]{:S(2)}) collective-permute-start(bf16[8,64]{1,0:T(8,128)(2,1)S(1)} %get-tuple-element.38), channel_id=1, source_target_pairs={{1,0},{3,2},{5,4},{7,6},{9,8},{11,10},{13,12},{15,14},{17,16},{19,... | collective-permute-start | bytes 3080 | tf_op jit(solution)/shard_map/ppermute | solution.py:17
  42.6 23.2 %collective-permute-start = (bf16[8,64]{1,0:T(8,128)(2,1)S(1)}, bf16[8,64]{1,0:T(8,128)(2,1)S(1)}, u32[]{:S(2)}, u32[]{:S(2)}) collective-permute-start(bf16[8,64]{1,0:T(8,128)(2,1)S(1)} %get-tuple-element.51), channel_id=1, source_target_pairs={{0,2},{2,4},{4,6},{6,8},{8,10},{10,12},{12,14},{14,16},{16,18},{18... | collective-permute-start | bytes 3080 | tf_op jit(solution)/shard_map/ppermute | solution.py:16
  43.9 21.9 %collective-permute-start.1 = (bf16[8,64]{1,0:T(8,128)(2,1)S(1)}, bf16[8,64]{1,0:T(8,128)(2,1)S(1)}, u32[]{:S(2)}, u32[]{:S(2)}) collective-permute-start(bf16[8,64]{1,0:T(8,128)(2,1)S(1)} %get-tuple-element.50), channel_id=1, source_target_pairs={{2,0},{4,2},{6,4},{8,6},{10,8},{12,10},{14,12},{16,14},{18,16},{20... | collective-permute-start | bytes 3080 | tf_op jit(solution)/shard_map/ppermute | solution.py:17
  46.2 19.6 %copy-start.7 = (bf16[2,3,3,64,64]{4,3,2,1,0:T(8,128)(2,1)S(1)}, bf16[2,3,3,64,64]{4,3,2,1,0:T(8,128)(2,1)}, u32[]{:S(2)}) copy-start(bf16[2,3,3,64,64]{4,3,2,1,0:T(8,128)(2,1)} %param.13) | copy-start | bytes 442372
  47.0 26.5 %collective-permute-start.8 = (bf16[64,8,256]{2,0,1:T(8,128)(2,1)}, bf16[64,8,256]{2,0,1:T(8,128)(2,1)}, u32[]{:S(2)}, u32[]{:S(2)}) collective-permute-start(bf16[64,8,256]{2,0,1:T(8,128)(2,1)} %copy.143), channel_id=1, source_target_pairs={{0,2},{2,4},{4,6},{6,8},{8,10},{10,12},{12,14},{14,16},{16,18},{18... | collective-permute-start | bytes 786440 | tf_op jit(solution)/shard_map/ppermute | solution.py:16
  64.3 2.7 copy-start.13
  64.3 10.3 %collective-permute-start.9 = (bf16[64,8,256]{2,0,1:T(8,128)(2,1)}, bf16[64,8,256]{2,0,1:T(8,128)(2,1)S(1)}, u32[]{:S(2)}, u32[]{:S(2)}) collective-permute-start(bf16[64,8,256]{2,0,1:T(8,128)(2,1)} %copy.144), channel_id=1, source_target_pairs={{2,0},{4,2},{6,4},{8,6},{10,8},{12,10},{14,12},{16,14},{18,16},{20... | collective-permute-start | bytes 786440 | tf_op jit(solution)/shard_map/ppermute | solution.py:17
  68.4 4.8 %copy-start.4 = (bf16[3,3,64,64]{3,2,1,0:T(8,128)(2,1)S(1)}, bf16[3,3,64,64]{3,2,1,0:T(8,128)(2,1)}, u32[]{:S(2)}) copy-start(bf16[3,3,64,64]{3,2,1,0:T(8,128)(2,1)} %param.15) | copy-start | bytes 221188
  68.8 11.5 %collective-permute-start.4 = (bf16[64,8,256]{2,0,1:T(8,128)(2,1)S(1)}, bf16[64,8,256]{2,0,1:T(8,128)(2,1)S(1)}, u32[]{:S(2)}, u32[]{:S(2)}) collective-permute-start(bf16[64,8,256]{2,0,1:T(8,128)(2,1)S(1)} %get-tuple-element.26), channel_id=1, source_target_pairs={{0,2},{2,4},{4,6},{6,8},{8,10},{10,12},{12,14},{14,16},{16,18},{18... | collective-permute-start | bytes 786440 | tf_op jit(solution)/shard_map/ppermute | solution.py:16
  71.8 8.5 %collective-permute-start.5 = (bf16[64,8,256]{2,0,1:T(8,128)(2,1)S(1)}, bf16[64,8,256]{2,0,1:T(8,128)(2,1)S(1)}, u32[]{:S(2)}, u32[]{:S(2)}) collective-permute-start(bf16[64,8,256]{2,0,1:T(8,128)(2,1)S(1)} %get-tuple-element.27), channel_id=1, source_target_pairs={{2,0},{4,2},{6,4},{8,6},{10,8},{12,10},{14,12},{16,14},{18,16},{20... | collective-permute-start | bytes 786440 | tf_op jit(solution)/shard_map/ppermute | solution.py:17
  75.0 15.6 %collective-permute-start.10 = (bf16[64,32,8]{2,0,1:T(8,128)(2,1)S(1)}, bf16[64,32,8]{2,0,1:T(8,128)(2,1)S(1)}, u32[]{:S(2)}, u32[]{:S(2)}) collective-permute-start(bf16[64,32,8]{2,0,1:T(8,128)(2,1)S(1)} %get-tuple-element.20), channel_id=1, source_target_pairs={{0,1},{2,3},{4,5},{6,7},{8,9},{10,11},{12,13},{14,15},{16,17},{18,... | collective-permute-start | bytes 98312 | tf_op jit(solution)/shard_map/ppermute | solution.py:16
  79.0 16.3 %collective-permute-start.11 = (bf16[64,32,8]{2,0,1:T(8,128)(2,1)S(1)}, bf16[64,32,8]{2,0,1:T(8,128)(2,1)S(1)}, u32[]{:S(2)}, u32[]{:S(2)}) collective-permute-start(bf16[64,32,8]{2,0,1:T(8,128)(2,1)S(1)} %get-tuple-element.21), channel_id=1, source_target_pairs={{1,0},{3,2},{5,4},{7,6},{9,8},{11,10},{13,12},{15,14},{17,16},{19,... | collective-permute-start | bytes 98312 | tf_op jit(solution)/shard_map/ppermute | solution.py:17
  80.3 1.4 copy-start.2
  81.7 82.2 %collective-permute-start.6 = (bf16[64,32,8]{2,0,1:T(8,128)(2,1)}, bf16[64,32,8]{2,0,1:T(8,128)(2,1)}, u32[]{:S(2)}, u32[]{:S(2)}) collective-permute-start(bf16[64,32,8]{2,0,1:T(8,128)(2,1)} %get-tuple-element.22), channel_id=1, source_target_pairs={{0,1},{2,3},{4,5},{6,7},{8,9},{10,11},{12,13},{14,15},{16,17},{18,... | collective-permute-start | bytes 98312 | tf_op jit(solution)/shard_map/ppermute | solution.py:16
  87.1 76.8 %collective-permute-start.7 = (bf16[64,32,8]{2,0,1:T(8,128)(2,1)}, bf16[64,32,8]{2,0,1:T(8,128)(2,1)}, u32[]{:S(2)}, u32[]{:S(2)}) collective-permute-start(bf16[64,32,8]{2,0,1:T(8,128)(2,1)} %get-tuple-element.23), channel_id=1, source_target_pairs={{1,0},{3,2},{5,4},{7,6},{9,8},{11,10},{13,12},{15,14},{17,16},{19,... | collective-permute-start | bytes 98312 | tf_op jit(solution)/shard_map/ppermute | solution.py:17
  102.8 61.1 %copy-start.3 = (bf16[64,8,256]{2,0,1:T(8,128)(2,1)S(1)}, bf16[64,8,256]{2,0,1:T(8,128)(2,1)}, u32[]{:S(2)}) copy-start(bf16[64,8,256]{2,0,1:T(8,128)(2,1)} %copy-done.2) | copy-start | bytes 786436
  102.8 236.8 %all-reduce.6.cloned.1.call-start = ((), (), s32[]{:S(2)}) async-start(), calls=%async_computation.1 | async-start | bytes 2031616 | tf_op jit(solution)/shard_map/psum | solution.py:239
  113.1 62.3 %collective-permute-start.12 = (f32[3,8,64]{2,1,0:T(8,128)S(1)}, f32[3,8,64]{2,1,0:T(8,128)S(1)}, u32[]{:S(2)}, u32[]{:S(2)}) collective-permute-start(f32[3,8,64]{2,1,0:T(8,128)S(1)} %get-tuple-element.43), channel_id=1, source_target_pairs={{0,2},{2,4},{4,6},{6,8},{8,10},{10,12},{12,14},{14,16},{16,18},{18... | collective-permute-start | bytes 18440 | tf_op jit(solution)/shard_map/ppermute | solution.py:16
  114.6 60.8 %collective-permute-start.13 = (f32[3,8,64]{2,1,0:T(8,128)S(1)}, f32[3,8,64]{2,1,0:T(8,128)S(1)}, u32[]{:S(2)}, u32[]{:S(2)}) collective-permute-start(f32[3,8,64]{2,1,0:T(8,128)S(1)} %get-tuple-element.44), channel_id=1, source_target_pairs={{2,0},{4,2},{6,4},{8,6},{10,8},{12,10},{14,12},{16,14},{18,16},{20... | collective-permute-start | bytes 18440 | tf_op jit(solution)/shard_map/ppermute | solution.py:17
  168.6 1.4 copy-start.5
  173.5 1.9 copy-start.11
  173.5 22.9 %copy-start.8 = (bf16[2,3,3,64,64]{4,3,2,1,0:T(8,128)(2,1)S(1)}, bf16[2,3,3,64,64]{4,3,2,1,0:T(8,128)(2,1)}, u32[]{:S(2)}) copy-start(bf16[2,3,3,64,64]{4,3,2,1,0:T(8,128)(2,1)} %param.13) | copy-start | bytes 442372
  197.7 10.6 %copy-start.10 = (bf16[16,256]{1,0:T(8,128)(2,1)S(1)}, bf16[16,256]{1,0:T(8,128)(2,1)}, u32[]{:S(2)}) copy-start(bf16[16,256]{1,0:T(8,128)(2,1)} %param.10) | copy-start | bytes 24580
  197.8 6.0 %collective-permute-start.14 = (f32[3,8,64]{1,2,0:T(8,128)S(1)}, f32[3,8,64]{1,2,0:T(8,128)S(1)}, u32[]{:S(2)}, u32[]{:S(2)}) collective-permute-start(f32[3,8,64]{1,2,0:T(8,128)S(1)} %get-tuple-element.31), channel_id=1, source_target_pairs={{0,1},{2,3},{4,5},{6,7},{8,9},{10,11},{12,13},{14,15},{16,17},{18,... | collective-permute-start | bytes 18440 | tf_op jit(solution)/shard_map/ppermute | solution.py:16
  201.3 6.6 %collective-permute-start.15 = (f32[3,8,64]{1,2,0:T(8,128)S(1)}, f32[3,8,64]{1,2,0:T(8,128)S(1)}, u32[]{:S(2)}, u32[]{:S(2)}) collective-permute-start(f32[3,8,64]{1,2,0:T(8,128)S(1)} %get-tuple-element.32), channel_id=1, source_target_pairs={{1,0},{3,2},{5,4},{7,6},{9,8},{11,10},{13,12},{15,14},{17,16},{19,... | collective-permute-start | bytes 18440 | tf_op jit(solution)/shard_map/ppermute | solution.py:17
  202.9 6.1 %copy-start.9 = (bf16[256,64]{0,1:T(8,128)(2,1)S(1)}, bf16[256,64]{0,1:T(8,128)(2,1)}, u32[]{:S(2)}) copy-start(bf16[256,64]{0,1:T(8,128)(2,1)} %param.11) | copy-start | bytes 98308
  339.6 5.1 %copy-start.6 = (f32[3,3,64,64]{3,2,1,0:T(8,128)S(1)}, f32[3,3,64,64]{3,2,1,0:T(8,128)}, u32[]{:S(2)}) copy-start(f32[3,3,64,64]{3,2,1,0:T(8,128)} %get-tuple-element.69) | copy-start | bytes 442372
Sparse Core Ops, SparseCore 0:
  102.9 92.3 all-reduce.3
  209.1 130.4 all-reduce.5
where the time goes:
time: 353 us; the launch traced here: 352 us
  waiting for transfers between devices  159 us (45%)
  blocking collectives  84.6 us (24%)
  starting transfers between devices  36.4 us (10%)
  matrix products  25.6 us (7%)
  between operations  24.7 us (7%)
  local copies, waits for them, and re-layouts  15.2 us (4%)
  other arithmetic  6.69 us (2%)
    psum x1, waiting for transfers between devices, shards(): lax.psum((grad_row_proj, grad_col_proj, jnp.stack([grad_row_pair, grad_co...  129 us
    psum x1, blocking collectives, shards(): lax.psum((grad_row_proj, grad_col_proj, jnp.stack([grad_row_pair, grad_co...  47.7 us
    ppermute x8, starting transfers between devices, padded_2(): before = lax.ppermute(last, axis, up)  25.9 us
    all_gather x1, blocking collectives, shards(): lax.all_gather(project(col_features, col_proj), 'row', axis=0, tiled=True)  23.3 us
    psum x1, waiting for transfers between devices, shards(): col_sums = lax.psum(col_part, 'row')  19 us
    ppermute x8, starting transfers between devices, padded_2(): after = lax.ppermute(leading, axis, down)  10.5 us
    unnamed x41, local copies, waits for them, and re-layouts  10.3 us
    ppermute x8, waiting for transfers between devices, padded_2(): after = lax.ppermute(leading, axis, down)  8.83 us
  transfers between devices with their start and end apart: 18, of which 5 were waited for; matrix products, arithmetic and copies ran while one was open for 10% of the time, Pallas kernels for 0%

commit v1 on v0

--- a/solution.py
+++ b/solution.py
@@ -133,7 +133,9 @@
     row_piece = row_features.shape[0]
     col_piece = col_features.shape[0]
     rows_a = lax.all_gather(project(row_features, row_proj), "col", axis=0, tiled=True)
-    cols_b = lax.all_gather(project(col_features, col_proj), "row", axis=0, tiled=True)
+    part = project(col_features, col_proj)
+    repeated = jnp.stack([part] * lax.axis_size("row"))
+    cols_b = jnp.concatenate(lax.all_to_all(repeated, "row", 0, 0), axis=0)
     pad_extra = 0
     a_pad = padded_2(rows_a, (("row", 0),), MAX_DILATION)
     b_pad = padded_2(cols_b, (("col", 0),), MAX_DILATION)

time: 353 us -> 346 us (0.980)
  blocking collectives: 84.6 us -> 60.9 us
  starting transfers between devices: 36.4 us -> 42.4 us
  matrix products: 25.6 us -> 30.2 us
  local copies, waits for them, and re-layouts: 15.2 us -> 18.8 us
    all_gather x1 -> x0, blocking collectives: 23.3 us -> none  [shards(): lax.all_gather(project(col_features, col_proj), 'row', axis=0, tiled=True)]
    psum x1, waiting for transfers between devices: 19 us -> 2.23 us  [shards(): col_sums = lax.psum(col_part, 'row')]
    ppermute x8, waiting for transfers between devices: 2 us -> 16.7 us  [padded_2(): before = lax.ppermute(last, axis, up)]
    ppermute x8, waiting for transfers between devices: 8.83 us -> 17.1 us  [padded_2(): after = lax.ppermute(leading, axis, down)]
    all_to_all x0 -> x1, starting transfers between devices: none -> 7.39 us  [shards(): cols_b = jnp.concatenate(lax.all_to_all(repeated, 'row', 0, 0), axis=0)]
    dot_general x9, matrix products: 3.75 us -> 9.43 us  [conv_taps(): jnp.einsum('co,cij->oij', weight[tap_row, tap_col], window, preferred_ele...]
    unnamed x41 -> x39, local copies, waits for them, and re-layouts: 10.3 us -> 11.6 us
  transfers between devices with their start and end apart: 18 -> 19, of which waited for: 5 -> 9; matrix products, arithmetic and copies ran while one was open for 10% -> 12% of each run, Pallas kernels for 0% -> 0%
where the time goes in v1:
time: 346 us; the launch traced here: 345 us
  waiting for transfers between devices  162 us (47%)
  blocking collectives  60.9 us (18%)
  starting transfers between devices  42.4 us (12%)
  matrix products  30.2 us (9%)
  between operations  24.6 us (7%)
  local copies, waits for them, and re-layouts  18.8 us (5%)
  other arithmetic  5.48 us (2%)
    psum x1, waiting for transfers between devices, shards(): lax.psum((grad_row_proj, grad_col_proj, jnp.stack([grad_row_pair, grad_co...  126 us
    psum x1, blocking collectives, shards(): lax.psum((grad_row_proj, grad_col_proj, jnp.stack([grad_row_pair, grad_co...  48 us
    ppermute x8, starting transfers between devices, padded_2(): before = lax.ppermute(last, axis, up)  24.6 us
    ppermute x8, waiting for transfers between devices, padded_2(): after = lax.ppermute(leading, axis, down)  17.1 us
    ppermute x8, waiting for transfers between devices, padded_2(): before = lax.ppermute(last, axis, up)  16.7 us
    unnamed x39, local copies, waits for them, and re-layouts  11.6 us
    ppermute x8, starting transfers between devices, padded_2(): after = lax.ppermute(leading, axis, down)  10.3 us
    dot_general x9, matrix products, conv_taps(): jnp.einsum('co,cij->oij', weight[tap_row, tap_col], window, preferred_ele...  9.43 us
  transfers between devices with their start and end apart: 19, of which 9 were waited for; matrix products, arithmetic and copies ran while one was open for 12% of the time, Pallas kernels for 0%

profile of v1, /device:TPU:0, one launch (start us, length us, event | category | flops | bytes accessed | tf_op | source)
XLA Modules:
  0.0 344.9 jit_solution(15591205327978352425)
XLA Ops:
  9.5 7.4 %all-to-all-start = ((bf16[16,2,512]{2,1,0:T(2,128)(2,1)}), bf16[16,2,512]{2,1,0:T(2,128)(2,1)S(1)}, u32[]{:S(2)}, u32[]{:S(2)}) async-start(bf16[16,2,512]{2,1,0:T(2,128)(2,1)} %reshape.186), calls=%async_computation | async-start | bytes 65536 | tf_op jit(solution)/shard_map/all_to_all | solution.py:138
  17.8 4.4 %all_gather.3 = bf16[16,64]{1,0:T(8,128)(2,1)S(1)} all-gather(bf16[8,64]{1,0:T(8,128)(2,1)S(1)} %convolution_convert_fusion.1), channel_id=1, replica_groups=mesh['row'=16,'col'=2] {'col'}, dimensions={0}, use_global_device_ids=true | all-gather | bytes 3072 | tf_op jit(solution)/shard_map/all_gather | solution.py:135
  22.2 1.4 collective-permute-start
  23.6 1.3 collective-permute-start.1
  24.9 1.1 fusion.195
  26.7 5.8 %collective-permute-start.8 = (bf16[64,8,256]{2,0,1:T(8,128)(2,1)}, bf16[64,8,256]{2,0,1:T(8,128)(2,1)}, u32[]{:S(2)}, u32[]{:S(2)}) collective-permute-start(bf16[64,8,256]{2,0,1:T(8,128)(2,1)} %copy.143), channel_id=1, source_target_pairs={{0,2},{2,4},{4,6},{6,8},{8,10},{10,12},{12,14},{14,16},{16,18},{18... | collective-permute-start | bytes 786440 | tf_op jit(solution)/shard_map/ppermute | solution.py:16
  33.3 1.3 collective-permute-start.9
  46.3 1.3 fusion.85
  48.0 3.4 collective-permute-start.2
  51.5 1.3 collective-permute-start.3
  52.8 4.1 %collective-permute-done.3 = bf16[8,64]{1,0:T(8,128)(2,1)S(1)} collective-permute-done((bf16[8,64]{1,0:T(8,128)(2,1)S(1)}, bf16[8,64]{1,0:T(8,128)(2,1)S(1)}, u32[]{:S(2)}, u32[]{:S(2)}) %collective-permute-start.3) | collective-permute-done | bytes 1056 | tf_op jit(solution)/shard_map/ppermute | solution.py:17
  57.9 1.3 multiply_convert_fusion
  60.4 2.2 collective-permute-start.4
  62.5 1.3 collective-permute-start.5
  63.8 1.3 fusion.87
  66.3 1.0 constant_dynamic-update-slice_fusion.3
  67.5 2.0 collective-permute-start.10
  69.5 1.3 collective-permute-start.11
  70.9 8.4 %collective-permute-done.10 = bf16[64,32,8]{2,0,1:T(8,128)(2,1)S(1)} collective-permute-done((bf16[64,32,8]{2,0,1:T(8,128)(2,1)S(1)}, bf16[64,32,8]{2,0,1:T(8,128)(2,1)S(1)}, u32[]{:S(2)}, u32[]{:S(2)}) %collective-permute-start.10) | collective-permute-done | bytes 32800 | tf_op jit(solution)/shard_map/ppermute | solution.py:16
  79.3 4.7 %collective-permute-done.11 = bf16[64,32,8]{2,0,1:T(8,128)(2,1)S(1)} collective-permute-done((bf16[64,32,8]{2,0,1:T(8,128)(2,1)S(1)}, bf16[64,32,8]{2,0,1:T(8,128)(2,1)S(1)}, u32[]{:S(2)}, u32[]{:S(2)}) %collective-permute-start.11) | collective-permute-done | bytes 32800 | tf_op jit(solution)/shard_map/ppermute | solution.py:17
  84.0 1.0 pad_maximum_fusion.1
  88.3 1.0 fusion.204
  89.3 1.8 convolution_bitcast_fusion.7
  92.0 8.5 %psum.49 = f32[3,16,64]{1,0,2:T(4,128)S(1)} all-reduce(f32[3,16,64]{1,0,2:T(4,128)S(1)} %bitcast.309), channel_id=1, replica_groups=mesh['row'=16,'col'=2] {'col'}, use_global_device_ids=true, to_apply=%region_0.1 | all-reduce | flops 3072 | bytes 24576 | tf_op jit(solution)/shard_map/psum | solution.py:171
  101.1 2.2 collective-permute-start.12
  103.3 1.3 collective-permute-start.13
  104.9 48.0 %psum.54 = f32[64]{0:T(128)} all-reduce(f32[64]{0:T(128)S(1)} %get-tuple-element.56), channel_id=1, replica_groups=mesh['row'=16,'col'=2] {'row','col'}, use_global_device_ids=true, to_apply=%region_6.7 | all-reduce | flops 64 | bytes 512 | tf_op jit(solution)/shard_map/psum | solution.py:241
  154.2 4.4 %collective-permute-start.6 = (bf16[64,32,8]{2,0,1:T(8,128)(2,1)S(1)}, bf16[64,32,8]{2,0,1:T(8,128)(2,1)S(1)}, u32[]{:S(2)}, u32[]{:S(2)}) collective-permute-start(bf16[64,32,8]{2,0,1:T(8,128)(2,1)S(1)} %get-tuple-element.22), channel_id=1, source_target_pairs={{0,1},{2,3},{4,5},{6,7},{8,9},{10,11},{12,13},{14,15},{16,17},{18,... | collective-permute-start | bytes 98312 | tf_op jit(solution)/shard_map/ppermute | solution.py:16
  158.6 1.3 collective-permute-start.7
  160.7 8.1 %collective-permute-done.6 = bf16[64,32,8]{2,0,1:T(8,128)(2,1)S(1)} collective-permute-done((bf16[64,32,8]{2,0,1:T(8,128)(2,1)S(1)}, bf16[64,32,8]{2,0,1:T(8,128)(2,1)S(1)}, u32[]{:S(2)}, u32[]{:S(2)}) %collective-permute-start.6) | collective-permute-done | bytes 32800 | tf_op jit(solution)/shard_map/ppermute | solution.py:16
  168.7 4.1 %collective-permute-done.7 = bf16[64,32,8]{2,0,1:T(8,128)(2,1)S(1)} collective-permute-done((bf16[64,32,8]{2,0,1:T(8,128)(2,1)S(1)}, bf16[64,32,8]{2,0,1:T(8,128)(2,1)S(1)}, u32[]{:S(2)}, u32[]{:S(2)}) %collective-permute-start.7) | collective-permute-done | bytes 32800 | tf_op jit(solution)/shard_map/ppermute | solution.py:17
  172.9 1.0 pad_maximum_fusion
  178.8 1.4 fusion.49
  180.2 1.4 fusion.35
  181.5 1.4 fusion.46
  184.1 2.2 all-reduce.4.cloned.1.call-done
  186.4 1.7 constant_dynamic-slice_fusion.3
  188.1 1.0 copy.47
  189.0 1.3 convolution_bitcast_fusion.8
  190.4 3.3 collective-permute-start.14
  193.8 1.3 collective-permute-start.15
  196.5 4.1 %collective-permute-done.15 = f32[3,8,64]{1,2,0:T(8,128)S(1)} collective-permute-done((f32[3,8,64]{1,2,0:T(8,128)S(1)}, f32[3,8,64]{1,2,0:T(8,128)S(1)}, u32[]{:S(2)}, u32[]{:S(2)}) %collective-permute-start.15) | collective-permute-done | bytes 6176 | tf_op jit(solution)/shard_map/ppermute | solution.py:17
  201.7 2.4 fusion.21
  204.0 1.1 copy.58
  205.9 126.3 %all-reduce.6.cloned.1.call-done = (f32[256,64]{0,1:T(8,128)}, f32[256,64]{0,1:T(8,128)}, f32[2,3,3,64,64]{3,4,1,2,0:T(8,128)}, f32[3,3,64,64]{3,2,1,0:T(8,128)}) async-done(((f32[256,64]{0,1:T(8,128)}, f32[256,64]{0,1:T(8,128)}, f32[2,3,3,64,64]{3,4,1,2,0:T(8,128)}, f32[3,3,64,64]{3,2,1,0:T(8,128)}), (f32[256,64]{0,1:T(8,128)}, f32[256,64]{0,1:T(8,128)}, f32[2,3,3,64,64]{3,4,1,2,0:T(8,128)}, ...) | async-done | bytes 573456 | tf_op jit(solution)/shard_map/psum | solution.py:241
  332.2 2.1 copy.59
  334.4 1.5 copy.156
  335.8 1.5 copy.157
  (117 shorter events, 27.4 us)
Async XLA Ops:
  7.2 0.8 copy-start
  7.2 39.1 %copy-start.1 = (bf16[64,16,256]{2,1,0:T(8,128)(2,1)S(1)}, bf16[64,16,256]{2,1,0:T(8,128)(2,1)}, u32[]{:S(2)}) copy-start(bf16[64,16,256]{2,1,0:T(8,128)(2,1)} %param.17) | copy-start | bytes 1572868
  7.2 27.4 %copy-start.11 = (s32[2]{0:T(128)S(1)}, s32[2]{0:T(128)}, u32[]{:S(2)}) copy-start(s32[2]{0:T(128)} %param.16) | copy-start | bytes 28
  7.2 39.1 %copy-start.4 = (bf16[3,3,64,64]{3,2,1,0:T(8,128)(2,1)S(1)}, bf16[3,3,64,64]{3,2,1,0:T(8,128)(2,1)}, u32[]{:S(2)}) copy-start(bf16[3,3,64,64]{3,2,1,0:T(8,128)(2,1)} %param.15) | copy-start | bytes 221188
  9.5 38.4 %all-to-all-start = ((bf16[16,2,512]{2,1,0:T(2,128)(2,1)}), bf16[16,2,512]{2,1,0:T(2,128)(2,1)S(1)}, u32[]{:S(2)}, u32[]{:S(2)}) async-start(bf16[16,2,512]{2,1,0:T(2,128)(2,1)} %reshape.186), calls=%async_computation | async-start | bytes 65536 | tf_op jit(solution)/shard_map/all_to_all | solution.py:138
  16.9 169.5 %all-reduce.4.cloned.1.call-start = ((), (), s32[]{:S(2)}) async-start(), calls=%async_computation.1 | async-start | bytes 524288 | tf_op jit(solution)/shard_map/psum | solution.py:172
  22.2 25.4 %collective-permute-start = (bf16[8,64]{1,0:T(8,128)(2,1)S(1)}, bf16[8,64]{1,0:T(8,128)(2,1)S(1)}, u32[]{:S(2)}, u32[]{:S(2)}) collective-permute-start(bf16[8,64]{1,0:T(8,128)(2,1)S(1)} %get-tuple-element.51), channel_id=1, source_target_pairs={{0,2},{2,4},{4,6},{6,8},{8,10},{10,12},{12,14},{14,16},{16,18},{18... | collective-permute-start | bytes 3080 | tf_op jit(solution)/shard_map/ppermute | solution.py:16
  23.6 24.1 %collective-permute-start.1 = (bf16[8,64]{1,0:T(8,128)(2,1)S(1)}, bf16[8,64]{1,0:T(8,128)(2,1)S(1)}, u32[]{:S(2)}, u32[]{:S(2)}) collective-permute-start(bf16[8,64]{1,0:T(8,128)(2,1)S(1)} %get-tuple-element.50), channel_id=1, source_target_pairs={{2,0},{4,2},{6,4},{8,6},{10,8},{12,10},{14,12},{16,14},{18,16},{20... | collective-permute-start | bytes 3080 | tf_op jit(solution)/shard_map/ppermute | solution.py:17
  25.9 21.8 %copy-start.7 = (bf16[2,3,3,64,64]{4,3,2,1,0:T(8,128)(2,1)S(1)}, bf16[2,3,3,64,64]{4,3,2,1,0:T(8,128)(2,1)}, u32[]{:S(2)}) copy-start(bf16[2,3,3,64,64]{4,3,2,1,0:T(8,128)(2,1)} %param.13) | copy-start | bytes 442372
  26.7 38.4 %collective-permute-start.8 = (bf16[64,8,256]{2,0,1:T(8,128)(2,1)}, bf16[64,8,256]{2,0,1:T(8,128)(2,1)}, u32[]{:S(2)}, u32[]{:S(2)}) collective-permute-start(bf16[64,8,256]{2,0,1:T(8,128)(2,1)} %copy.143), channel_id=1, source_target_pairs={{0,2},{2,4},{4,6},{6,8},{8,10},{10,12},{12,14},{14,16},{16,18},{18... | collective-permute-start | bytes 786440 | tf_op jit(solution)/shard_map/ppermute | solution.py:16
  33.3 33.0 %collective-permute-start.9 = (bf16[64,8,256]{2,0,1:T(8,128)(2,1)}, bf16[64,8,256]{2,0,1:T(8,128)(2,1)}, u32[]{:S(2)}, u32[]{:S(2)}) collective-permute-start(bf16[64,8,256]{2,0,1:T(8,128)(2,1)} %copy.144), channel_id=1, source_target_pairs={{2,0},{4,2},{6,4},{8,6},{10,8},{12,10},{14,12},{16,14},{18,16},{20... | collective-permute-start | bytes 786440 | tf_op jit(solution)/shard_map/ppermute | solution.py:17
  47.6 10.3 %copy-start.12 = (f32[64]{0:T(128)S(1)}, f32[64]{0:T(128)}, u32[]{:S(2)}) copy-start(f32[64]{0:T(128)} %param.14) | copy-start | bytes 772
  48.0 4.8 %collective-permute-start.2 = (bf16[8,64]{1,0:T(8,128)(2,1)S(1)}, bf16[8,64]{1,0:T(8,128)(2,1)S(1)}, u32[]{:S(2)}, u32[]{:S(2)}) collective-permute-start(bf16[8,64]{1,0:T(8,128)(2,1)S(1)} %get-tuple-element.38), channel_id=1, source_target_pairs={{0,1},{2,3},{4,5},{6,7},{8,9},{10,11},{12,13},{14,15},{16,17},{18,... | collective-permute-start | bytes 3080 | tf_op jit(solution)/shard_map/ppermute | solution.py:16
  51.5 5.5 %collective-permute-start.3 = (bf16[8,64]{1,0:T(8,128)(2,1)S(1)}, bf16[8,64]{1,0:T(8,128)(2,1)S(1)}, u32[]{:S(2)}, u32[]{:S(2)}) collective-permute-start(bf16[8,64]{1,0:T(8,128)(2,1)S(1)} %get-tuple-element.39), channel_id=1, source_target_pairs={{1,0},{3,2},{5,4},{7,6},{9,8},{11,10},{13,12},{15,14},{17,16},{19,... | collective-permute-start | bytes 3080 | tf_op jit(solution)/shard_map/ppermute | solution.py:17
  60.4 93.4 %collective-permute-start.4 = (bf16[64,8,256]{2,0,1:T(8,128)(2,1)}, bf16[64,8,256]{2,0,1:T(8,128)(2,1)S(1)}, u32[]{:S(2)}, u32[]{:S(2)}) collective-permute-start(bf16[64,8,256]{2,0,1:T(8,128)(2,1)} %get-tuple-element.26), channel_id=1, source_target_pairs={{0,2},{2,4},{4,6},{6,8},{8,10},{10,12},{12,14},{14,16},{16,18},{18... | collective-permute-start | bytes 786440 | tf_op jit(solution)/shard_map/ppermute | solution.py:16
  62.5 91.3 %collective-permute-start.5 = (bf16[64,8,256]{2,0,1:T(8,128)(2,1)S(1)}, bf16[64,8,256]{2,0,1:T(8,128)(2,1)S(1)}, u32[]{:S(2)}, u32[]{:S(2)}) collective-permute-start(bf16[64,8,256]{2,0,1:T(8,128)(2,1)S(1)} %get-tuple-element.27), channel_id=1, source_target_pairs={{2,0},{4,2},{6,4},{8,6},{10,8},{12,10},{14,12},{16,14},{18,16},{20... | collective-permute-start | bytes 786440 | tf_op jit(solution)/shard_map/ppermute | solution.py:17
  67.5 11.7 %collective-permute-start.10 = (bf16[64,32,8]{2,0,1:T(8,128)(2,1)S(1)}, bf16[64,32,8]{2,0,1:T(8,128)(2,1)S(1)}, u32[]{:S(2)}, u32[]{:S(2)}) collective-permute-start(bf16[64,32,8]{2,0,1:T(8,128)(2,1)S(1)} %get-tuple-element.20), channel_id=1, source_target_pairs={{0,1},{2,3},{4,5},{6,7},{8,9},{10,11},{12,13},{14,15},{16,17},{18,... | collective-permute-start | bytes 98312 | tf_op jit(solution)/shard_map/ppermute | solution.py:16
  69.5 14.5 %collective-permute-start.11 = (bf16[64,32,8]{2,0,1:T(8,128)(2,1)S(1)}, bf16[64,32,8]{2,0,1:T(8,128)(2,1)S(1)}, u32[]{:S(2)}, u32[]{:S(2)}) collective-permute-start(bf16[64,32,8]{2,0,1:T(8,128)(2,1)S(1)} %get-tuple-element.21), channel_id=1, source_target_pairs={{1,0},{3,2},{5,4},{7,6},{9,8},{11,10},{13,12},{15,14},{17,16},{19,... | collective-permute-start | bytes 98312 | tf_op jit(solution)/shard_map/ppermute | solution.py:17
  86.6 1.2 copy-start.3
  91.1 61.9 %copy-start.10 = (bf16[8,256]{1,0:T(8,128)(2,1)S(1)}, bf16[8,256]{1,0:T(8,128)(2,1)}, u32[]{:S(2)}) copy-start(bf16[8,256]{1,0:T(8,128)(2,1)} %param.9) | copy-start | bytes 12292
  91.8 240.4 %all-reduce.6.cloned.1.call-start = ((), (), s32[]{:S(2)}) async-start(), calls=%async_computation.2 | async-start | bytes 2031616 | tf_op jit(solution)/shard_map/psum | solution.py:241
  101.1 51.8 %collective-permute-start.12 = (f32[3,8,64]{2,1,0:T(8,128)S(1)}, f32[3,8,64]{2,1,0:T(8,128)S(1)}, u32[]{:S(2)}, u32[]{:S(2)}) collective-permute-start(f32[3,8,64]{2,1,0:T(8,128)S(1)} %get-tuple-element.43), channel_id=1, source_target_pairs={{0,2},{2,4},{4,6},{6,8},{8,10},{10,12},{12,14},{14,16},{16,18},{18... | collective-permute-start | bytes 18440 | tf_op jit(solution)/shard_map/ppermute | solution.py:16
  103.3 49.6 %collective-permute-start.13 = (f32[3,8,64]{2,1,0:T(8,128)S(1)}, f32[3,8,64]{2,1,0:T(8,128)S(1)}, u32[]{:S(2)}, u32[]{:S(2)}) collective-permute-start(f32[3,8,64]{2,1,0:T(8,128)S(1)} %get-tuple-element.44), channel_id=1, source_target_pairs={{2,0},{4,2},{6,4},{8,6},{10,8},{12,10},{14,12},{16,14},{18,16},{20... | collective-permute-start | bytes 18440 | tf_op jit(solution)/shard_map/ppermute | solution.py:17
  153.9 6.0 %copy-start.8 = (bf16[256,64]{0,1:T(8,128)(2,1)S(1)}, bf16[256,64]{0,1:T(8,128)(2,1)}, u32[]{:S(2)}) copy-start(bf16[256,64]{0,1:T(8,128)(2,1)} %param.11) | copy-start | bytes 98308
  154.2 14.5 %collective-permute-start.6 = (bf16[64,32,8]{2,0,1:T(8,128)(2,1)S(1)}, bf16[64,32,8]{2,0,1:T(8,128)(2,1)S(1)}, u32[]{:S(2)}, u32[]{:S(2)}) collective-permute-start(bf16[64,32,8]{2,0,1:T(8,128)(2,1)S(1)} %get-tuple-element.22), channel_id=1, source_target_pairs={{0,1},{2,3},{4,5},{6,7},{8,9},{10,11},{12,13},{14,15},{16,17},{18,... | collective-permute-start | bytes 98312 | tf_op jit(solution)/shard_map/ppermute | solution.py:16
  158.6 14.2 %collective-permute-start.7 = (bf16[64,32,8]{2,0,1:T(8,128)(2,1)S(1)}, bf16[64,32,8]{2,0,1:T(8,128)(2,1)S(1)}, u32[]{:S(2)}, u32[]{:S(2)}) collective-permute-start(bf16[64,32,8]{2,0,1:T(8,128)(2,1)S(1)} %get-tuple-element.23), channel_id=1, source_target_pairs={{1,0},{3,2},{5,4},{7,6},{9,8},{11,10},{13,12},{15,14},{17,16},{19,... | collective-permute-start | bytes 98312 | tf_op jit(solution)/shard_map/ppermute | solution.py:17
  176.2 1.4 copy-start.5
  180.1 2.8 copy-start.2
  190.3 10.6 %copy-start.9 = (bf16[16,256]{1,0:T(8,128)(2,1)S(1)}, bf16[16,256]{1,0:T(8,128)(2,1)}, u32[]{:S(2)}) copy-start(bf16[16,256]{1,0:T(8,128)(2,1)} %param.10) | copy-start | bytes 24580
  190.4 6.0 %collective-permute-start.14 = (f32[3,8,64]{1,2,0:T(8,128)S(1)}, f32[3,8,64]{1,2,0:T(8,128)S(1)}, u32[]{:S(2)}, u32[]{:S(2)}) collective-permute-start(f32[3,8,64]{1,2,0:T(8,128)S(1)} %get-tuple-element.31), channel_id=1, source_target_pairs={{0,1},{2,3},{4,5},{6,7},{8,9},{10,11},{12,13},{14,15},{16,17},{18,... | collective-permute-start | bytes 18440 | tf_op jit(solution)/shard_map/ppermute | solution.py:16
  193.8 6.8 %collective-permute-start.15 = (f32[3,8,64]{1,2,0:T(8,128)S(1)}, f32[3,8,64]{1,2,0:T(8,128)S(1)}, u32[]{:S(2)}, u32[]{:S(2)}) collective-permute-start(f32[3,8,64]{1,2,0:T(8,128)S(1)} %get-tuple-element.32), channel_id=1, source_target_pairs={{1,0},{3,2},{5,4},{7,6},{9,8},{11,10},{13,12},{15,14},{17,16},{19,... | collective-permute-start | bytes 18440 | tf_op jit(solution)/shard_map/ppermute | solution.py:17
  332.2 5.1 %copy-start.6 = (f32[3,3,64,64]{3,2,1,0:T(8,128)S(1)}, f32[3,3,64,64]{3,2,1,0:T(8,128)}, u32[]{:S(2)}) copy-start(f32[3,3,64,64]{3,2,1,0:T(8,128)} %get-tuple-element.69) | copy-start | bytes 442372
Sparse Core Ops, SparseCore 0:
  92.0 94.3 all-reduce.3
  201.8 130.3 all-reduce.5
